TPU v7x, 512 devices: a whole 4x8x8 slice. The times are simulated.
512 devices in a mesh: row: 32 (over z_lo, y, core), col: 16 (over z_hi, x).
Axes of the slice: x: 4, y: 8, z: 8 (z_hi: 4, z_lo: 2; z = z_hi * 2 + z_lo), core: 2. Of those that a mesh axis runs over, the one named last changes fastest.
Arguments:
- phase: float32 [6, 524288], P(None, ('col', 'row')), may hold values from -6 to 6
- mass: float32 [524288], P(('col', 'row')), may hold values from 0.2 to 5
- active: int32 [4096], P(('row', 'col')), may hold values from 0 to 524287, as said below
Outputs:
- accels: float32 [3, 4096], P(None, ('row', 'col'))
- jerks: float32 [3, 4096], P(None, ('row', 'col'))
Inputs may be any that keep to these rules, and one draw needn't show every extreme that they name: `active`: the 4096 indices are distinct.
All inputs are finite; a program needn't handle non-finite values.
Results may differ from a plain program's by a relative error of at most 0.0003.
Values sent between devices are 32-bit elements; how exact they have to be, the bound alone decides.
A program may use at most 64 MiB of HBM per device.

v0:
```python
import math
import jax
import jax.numpy as jnp
from jax import lax
from jax.sharding import PartitionSpec as P

SOFTENING = 0.0001


def pair_terms(targets, src_phase, src_mass):
    offset = src_phase[0:3, None, :] - targets[0:3, :, None]
    vel_diff = src_phase[3:6, None, :] - targets[3:6, :, None]
    dist_sq = jnp.sum(offset * offset, axis=0) + SOFTENING
    inverse = lax.rsqrt(dist_sq)
    inverse_sq = inverse * inverse
    weight = src_mass[None, :] * inverse * inverse_sq
    radial = 3.0 * jnp.sum(offset * vel_diff, axis=0) * inverse_sq
    accels = jnp.sum(weight[None] * offset, axis=-1)
    jerks = jnp.sum(weight[None] * (vel_diff - radial[None] * offset), axis=-1)
    return (accels, jerks)


def select_stars(source, indices, first):
    columns = source.shape[1]
    offsets = indices - first
    inside = ((offsets >= 0) & (offsets < columns)).astype(jnp.float32)
    picked = jnp.take(source, jnp.clip(offsets, 0, columns - 1), axis=1)
    return picked * inside[None, :]


def sweep_sources(targets, src_phase, src_mass):
    columns = src_phase.shape[1]
    block_len = math.gcd(columns, 2048)

    def add_block(counter, carry):
        first = counter * block_len
        piece = lax.dynamic_slice_in_dim(src_phase, first, block_len, 1)
        masses = lax.dynamic_slice_in_dim(src_mass, first, block_len, 0)
        accels, jerks = pair_terms(targets, piece, masses)
        return (carry[0] + accels, carry[1] + jerks)

    zeros = jnp.zeros((3, targets.shape[1]), jnp.float32)
    return lax.fori_loop(0, columns // block_len, add_block, (zeros, zeros))


def shards(phase, mass, active):
    row_count = lax.axis_size("row")
    col_count = lax.axis_size("col")
    col_at = lax.axis_index("col")
    norming = 1.0 / (phase.shape[1] * row_count * col_count)
    block_ids = lax.all_gather(active, "col", axis=0, tiled=True)
    src_phase, src_mass = (
        lax.all_gather(phase, "row", axis=1, tiled=True),
        lax.all_gather(mass, "row", axis=0, tiled=True),
    )
    picked = select_stars(src_phase, block_ids, col_at * src_phase.shape[1])
    targets = lax.psum(picked, "col")
    accels, jerks = sweep_sources(targets, src_phase, src_mass)
    accels, jerks = (
        lax.psum_scatter(accels, "col", scatter_dimension=1, tiled=True),
        lax.psum_scatter(jerks, "col", scatter_dimension=1, tiled=True),
    )
    return (accels * norming, jerks * norming)


def solution(mesh):
    in_specs = (P(None, ("col", "row")), P(("col", "row")), P(("row", "col")))
    out_specs = (P(None, ("row", "col")), P(None, ("row", "col")))
    return jax.shard_map(shards, mesh=mesh, in_specs=in_specs, out_specs=out_specs, check_vma=False)
```

profile of v0, /device:TPU:2, one launch (start us, length us, event | category | flops | bytes accessed | tf_op | source)
XLA Modules:
  0.0 338.0 jit_solution(16159620314069810083)
XLA Ops:
  0.6 1.4 fusion.6
  3.5 22.6 %all-reduce = s32[128]{0:T(128)S(1)} all-reduce(s32[128]{0:T(128)S(1)} %dynamic-update-slice), channel_id=1, replica_groups=mesh['row'=32,'col'=16] {'col'}, use_global_device_ids=true, to_apply=%add | all-reduce | flops 128 | bytes 1024
  26.1 1.0 copy.11
  27.1 102.1 %all_gather.10 = f32[6,32768]{0,1:T(8,128)} all-gather(f32[6,1024]{0,1:T(8,128)S(1)} %copy.11), channel_id=1, replica_groups=mesh['row'=32,'col'=16] {'row'}, dimensions={1}, use_global_device_ids=true | all-gather | bytes 811008 | tf_op jit(solution)/shard_map/all_gather | solution.py:53
  129.2 6.4 %gather_fusion = f32[128,6]{1,0:T(8,128)S(1)} fusion(f32[6,32768]{0,1:T(8,128)} %all_gather.10, s32[1024]{0:T(1024)S(1)} %pad_clamp_fusion), kind=kCustom, calls=%fused_computation | custom fusion | bytes 6656 | tf_op jit(solution)/shard_map/jit(_take)/gather | solution.py:27
  135.7 73.9 %psum.7 = f32[6,128]{0,1:T(8,128)S(1)} all-reduce(f32[6,128]{0,1:T(8,128)S(1)} %multiply_bitcast_fusion), channel_id=1, replica_groups=mesh['row'=32,'col'=16] {'col'}, use_global_device_ids=true, to_apply=%region_0.1 | all-reduce | flops 768 | bytes 6144 | tf_op jit(solution)/shard_map/psum | solution.py:57
  209.7 9.9 %copy.12 = f32[6,32768]{1,0:T(8,128)S(1)} copy(f32[6,32768]{0,1:T(8,128)} %all_gather.10) | data formatting | bytes 1572864
  219.6 32.5 %all_gather.9 = f32[32768]{0:T(1024)S(1)} all-gather(f32[1024]{0:T(1024)S(1)} %copy-done), channel_id=1, replica_groups=mesh['row'=32,'col'=16] {'row'}, dimensions={0}, use_global_device_ids=true | all-gather | bytes 135168 | tf_op jit(solution)/shard_map/all_gather | solution.py:54
  252.1 40.6 %while.16 = (s32[]{:T(128)}, f32[3,128]{1,0:T(4,128)S(1)}, f32[3,128]{1,0:T(4,128)S(1)}, f32[32768]{0:T(1024)S(1)}, f32[6,32768]{1,0:T(8,128)S(1)}, /*index=5*/f...) while((s32[]{:T(128)}, f32[3,128]{1,0:T(4,128)S(1)}, ...), condition=%wide.region_6.7_spmd.clone, body=%wide.region_1.6_spmd.clone.sunk | while | flops 12059400 | bytes 8634557 | solution.py:43
  252.2 0.9 fusion.11
  253.4 1.2 fusion.12
  254.8 0.9 fusion.11
  256.0 1.2 fusion.12
  257.3 0.9 fusion.11
  258.5 1.2 fusion.12
  259.9 0.9 fusion.11
  261.1 1.2 fusion.12
  262.4 0.9 fusion.11
  263.6 1.2 fusion.12
  265.0 0.9 fusion.11
  266.1 1.2 fusion.12
  268.7 1.2 fusion.12
  271.2 1.2 fusion.12
  273.8 1.2 fusion.12
  276.3 1.2 fusion.12
  278.9 1.2 fusion.12
  281.4 1.2 fusion.12
  283.9 1.2 fusion.12
  286.5 1.2 fusion.12
  289.0 1.2 fusion.12
  291.6 1.2 fusion.12
  292.8 43.9 %all-reduce.3 = (f32[3,128]{1,0:T(4,128)S(1)}, f32[3,128]{1,0:T(4,128)S(1)}) all-reduce(f32[3,128]{1,0:T(4,128)S(1)} %get-tuple-element.112, f32[3,128]{1,0:T(4,128)S(1)} %get-tuple-element.113), channel_id=2, replica_groups=mesh['row'=32,'col'=16] {'col'}, use_global_device_ids=true, to_apply=%region_7.8.clone | all-reduce | flops 768 | bytes 6144
  (101 shorter events, 17.0 us)
Async XLA Ops:
  209.7 9.9 %copy-start = (f32[1024]{0:T(1024)S(1)}, f32[1024]{0:T(1024)}, u32[]{:S(2)}) copy-start(f32[1024]{0:T(1024)} %param.6) | copy-start | bytes 12292
where the time goes:
time: 338 us
  blocking collectives  275 us (81%)
  other arithmetic  38.7 us (11%)
  local copies, waits for them, and re-layouts  21.3 us (6%)
    all_gather x1, blocking collectives, shards(): lax.all_gather(phase, 'row', axis=1, tiled=True)  102 us
    psum x1, blocking collectives, shards(): targets = lax.psum(picked, 'col')  73.9 us
    unnamed x2, blocking collectives  66.4 us
    all_gather x1, blocking collectives, shards(): lax.all_gather(mass, 'row', axis=0, tiled=True)  32.5 us
    reduce_sum x16, other arithmetic, pair_terms(): jerks = jnp.sum(weight[None] * (vel_diff - radial[None] * offset), axis=-1)  19.2 us
    reduce_sum x16, other arithmetic, pair_terms(): radial = 3.0 * jnp.sum(offset * vel_diff, axis=0) * inverse_sq  13.7 us
    unnamed x7, local copies, waits for them, and re-layouts  13.2 us

commit v1 on v0

--- a/solution.py
+++ b/solution.py
@@ -50,7 +50,7 @@
     norming = 1.0 / (phase.shape[1] * row_count * col_count)
     block_ids = lax.all_gather(active, "col", axis=0, tiled=True)
     src_phase, src_mass = (
-        lax.all_gather(phase, "row", axis=1, tiled=True),
+        jnp.concatenate(lax.all_gather(phase, "row"), axis=1),
         lax.all_gather(mass, "row", axis=0, tiled=True),
     )
     picked = select_stars(src_phase, block_ids, col_at * src_phase.shape[1])

time: 338 us -> 280 us (0.83)
  the two profiles are of different devices: /device:TPU:2 before, /device:TPU:10 now
where the time goes in v1:
time: 280 us
  blocking collectives  209 us (75%)
  other arithmetic  38.7 us (14%)
  local copies, waits for them, and re-layouts  28.6 us (10%)
    psum x1, blocking collectives, shards(): targets = lax.psum(picked, 'col')  73.9 us
    unnamed x2, blocking collectives  66.5 us
    all_gather x1, blocking collectives, shards(): lax.all_gather(phase, 'row')  35.5 us
    all_gather x1, blocking collectives, shards(): lax.all_gather(mass, 'row', axis=0, tiled=True)  33.5 us
    reduce_sum x16, other arithmetic, pair_terms(): jerks = jnp.sum(weight[None] * (vel_diff - radial[None] * offset), axis=-1)  19.2 us
    reduce_sum x16, other arithmetic, pair_terms(): radial = 3.0 * jnp.sum(offset * vel_diff, axis=0) * inverse_sq  13.7 us
    unnamed x6, local copies, waits for them, and re-layouts  12.2 us
    reshape x1, local copies, waits for them, and re-layouts, shards(): jnp.concatenate(lax.all_gather(phase, 'row'), axis=1)  8.29 us

profile of v1, /device:TPU:10, one launch (start us, length us, event | category | flops | bytes accessed | tf_op | source)
XLA Modules:
  0.0 279.7 jit_solution(16788318567259979132)
XLA Ops:
  0.6 1.4 fusion.6
  3.5 22.6 %all-reduce = s32[128]{0:T(128)S(1)} all-reduce(s32[128]{0:T(128)S(1)} %dynamic-update-slice), channel_id=1, replica_groups=mesh['row'=32,'col'=16] {'col'}, use_global_device_ids=true, to_apply=%add | all-reduce | flops 128 | bytes 1024
  26.1 35.5 %all-gather.1 = f32[32,6,1024]{2,1,0:T(8,128)S(1)} all-gather(f32[1,6,1024]{2,1,0:T(8,128)} %bitcast.14), channel_id=2, replica_groups=mesh['row'=32,'col'=16] {'row'}, dimensions={0}, use_global_device_ids=true | all-gather | bytes 811008 | tf_op jit(solution)/shard_map/all_gather | solution.py:53
  61.6 8.3 %copy.11 = f32[6,32,1024]{0,2,1:T(8,128)} copy(f32[6,32,1024]{2,0,1:T(8,128)S(1)} %bitcast.13) | data formatting | bytes 1572864 | tf_op jit(solution)/shard_map/reshape | solution.py:53
  69.9 6.4 %gather_fusion = f32[128,6]{1,0:T(8,128)S(1)} fusion(f32[6,32768]{0,1:T(8,128)} %bitcast.11, s32[1024]{0:T(1024)S(1)} %pad_clamp_fusion), kind=kCustom, calls=%fused_computation | custom fusion | bytes 6656 | tf_op jit(solution)/shard_map/jit(_take)/gather | solution.py:27
  76.4 73.9 %psum.7 = f32[6,128]{0,1:T(8,128)S(1)} all-reduce(f32[6,128]{0,1:T(8,128)S(1)} %multiply_bitcast_fusion), channel_id=1, replica_groups=mesh['row'=32,'col'=16] {'col'}, use_global_device_ids=true, to_apply=%region_0.1 | all-reduce | flops 768 | bytes 6144 | tf_op jit(solution)/shard_map/psum | solution.py:57
  150.3 9.9 %copy.12 = f32[6,32768]{1,0:T(8,128)S(1)} copy(f32[6,32768]{0,1:T(8,128)} %bitcast.12) | data formatting | bytes 1572864
  160.3 33.5 %all_gather.12 = f32[32768]{0:T(1024)S(1)} all-gather(f32[1024]{0:T(1024)S(1)} %copy-done), channel_id=1, replica_groups=mesh['row'=32,'col'=16] {'row'}, dimensions={0}, use_global_device_ids=true | all-gather | bytes 135168 | tf_op jit(solution)/shard_map/all_gather | solution.py:54
  193.8 40.7 %while.16 = (s32[]{:T(128)}, f32[3,128]{1,0:T(4,128)S(1)}, f32[3,128]{1,0:T(4,128)S(1)}, f32[32768]{0:T(1024)S(1)}, f32[6,32768]{1,0:T(8,128)S(1)}, /*index=5*/f...) while((s32[]{:T(128)}, f32[3,128]{1,0:T(4,128)S(1)}, ...), condition=%wide.region_6.7_spmd.clone, body=%wide.region_1.6_spmd.clone.sunk | while | flops 12059400 | bytes 8634557 | solution.py:43
  193.9 0.9 fusion.11
  195.1 1.2 fusion.12
  196.4 0.9 fusion.11
  197.6 1.2 fusion.12
  199.0 0.9 fusion.11
  200.2 1.2 fusion.12
  201.5 0.9 fusion.11
  202.7 1.2 fusion.12
  204.1 0.9 fusion.11
  205.3 1.2 fusion.12
  206.6 0.9 fusion.11
  207.8 1.2 fusion.12
  210.4 1.2 fusion.12
  212.9 1.2 fusion.12
  215.4 1.2 fusion.12
  218.0 1.2 fusion.12
  220.5 1.2 fusion.12
  223.1 1.2 fusion.12
  225.6 1.2 fusion.12
  228.2 1.2 fusion.12
  230.7 1.2 fusion.12
  233.2 1.2 fusion.12
  234.5 43.9 %all-reduce.3 = (f32[3,128]{1,0:T(4,128)S(1)}, f32[3,128]{1,0:T(4,128)S(1)}) all-reduce(f32[3,128]{1,0:T(4,128)S(1)} %get-tuple-element.112, f32[3,128]{1,0:T(4,128)S(1)} %get-tuple-element.113), channel_id=3, replica_groups=mesh['row'=32,'col'=16] {'col'}, use_global_device_ids=true, to_apply=%region_7.8.clone | all-reduce | flops 768 | bytes 6144
  (101 shorter events, 17.0 us)
Async XLA Ops:
  150.3 9.9 %copy-start = (f32[1024]{0:T(1024)S(1)}, f32[1024]{0:T(1024)}, u32[]{:S(2)}) copy-start(f32[1024]{0:T(1024)} %param.6) | copy-start | bytes 12292
